TPU v7x, 32 devices: a whole 2x2x4 slice. The times are simulated.
32 devices in a mesh: pair: 4 (over x, core), blk: 8 (over z, y).
Axes of the slice: x: 2, y: 2, z: 4, core: 2. Of those that a mesh axis runs over, the one named last changes fastest.
Arguments:
- left_feats: bfloat16 [4, 64, 256, 256], P('pair', None, 'blk'), may hold values from -6 to 6
- right_feats: bfloat16 [4, 64, 256, 256], P('pair', None, 'blk'), may hold values from -6 to 6
- offsets: int32 [8], P('blk'), may hold values from 0 to 3, as said below
- hidden: bfloat16 [4, 64, 256, 128], P('pair', None, 'blk'), may hold values from -1 to 1
- context: bfloat16 [4, 3, 64, 256, 128], P('pair', None, None, 'blk'), may hold values from -6 to 6
- gru_weights: bfloat16 [2, 3, 5, 164, 128], replicated, may hold values from -0.21875 to 0.21875
- hidden_grad: float32 [4, 64, 256, 128], P('pair', None, 'blk'), may hold values from -0.06 to 0.06
Outputs:
- new_hidden: bfloat16 [4, 64, 256, 128], P('pair', None, 'blk')
- weight_grads: float32 [2, 3, 5, 164, 128], replicated
- hidden_in_grad: float32 [4, 64, 256, 128], P('pair', None, 'blk')
Inputs may be any that keep to these rules, and one draw needn't show every extreme that they name: Stripe s reads the frame-2 blocks s - offsets[s] - 1 and s - offsets[s]; some stripe has offset 4 - 1.
All inputs are finite; a program needn't handle non-finite values.
Results may differ from a plain program's by a relative error of at most 0.0054.
Values may be sent and summed in bfloat16 or wider, within the bound.
A program may use at most 128 MiB of HBM per device.

v0:
```python
import functools
import math
import jax
import jax.numpy as jnp
import numpy as np
from jax import lax
from jax.sharding import PartitionSpec as P

LEVELS = 4
RADIUS = 4


def with_halo(block, sides, width):
    for axis, dim in sides:
        count = lax.axis_size(axis)
        forward = [(i, i + 1) for i in range(count - 1)]
        backward = [(target, source) for source, target in forward]
        low = lax.ppermute(
            lax.slice_in_dim(block, block.shape[dim] - width, None, axis=dim), axis, forward
        )
        high = lax.ppermute(lax.slice_in_dim(block, 0, width, axis=dim), axis, backward)
        block = jnp.concatenate([low, block, high], axis=dim)
    return block


def lookup_table(column_count, level_count, radius_len):
    tap_count = 2 * radius_len + 1
    lookup = np.zeros((column_count, 2 * column_count, level_count * tap_count), np.float32)
    positions = np.arange(column_count)
    for level_id in range(level_count):
        pool_span = 2**level_id
        pooled_cols = 2 * column_count // pool_span
        for tap_id in range(tap_count):
            centre = (positions + column_count // 2) // pool_span + tap_id - radius_len
            inside = (centre >= 0) & (centre < pooled_cols)
            for inner_id in range(pool_span):
                lookup[
                    positions[inside],
                    centre[inside] * pool_span + inner_id,
                    level_id * tap_count + tap_id,
                ] = (1.0 / pool_span)
    return lookup


def tap_stack(padded, extent, axis_dim, kernel_len):
    return jnp.concatenate(
        [
            lax.slice_in_dim(padded, tap_id, tap_id + extent, axis=axis_dim)
            for tap_id in range(kernel_len)
        ],
        axis=-1,
    )


def conv_apply(padded, weight_taps, extent, axis_dim):
    kernel_len, in_chan, out_chan = weight_taps.shape
    stacked = tap_stack(padded, extent, axis_dim, kernel_len)
    flat_taps = stacked.reshape(-1, kernel_len * in_chan)
    result = jnp.dot(
        flat_taps,
        weight_taps.reshape(kernel_len * in_chan, out_chan),
        preferred_element_type=jnp.float32,
    )
    return result.reshape(stacked.shape[:-1] + (out_chan,))


def conv_weight_grad(padded, deltas, axis_dim):
    extent = deltas.shape[axis_dim]
    kernel_len = padded.shape[axis_dim] - extent + 1
    stacked = tap_stack(padded, extent, axis_dim, kernel_len)
    flat_taps = stacked.reshape(-1, stacked.shape[-1])
    flat_deltas = deltas.reshape(-1, deltas.shape[-1])
    result = lax.dot_general(
        flat_taps, flat_deltas, (((0,), (0,)), ((), ())), preferred_element_type=jnp.float32
    )
    return result.reshape(kernel_len, padded.shape[-1], deltas.shape[-1])


def conv_input_grad(deltas, weight_taps, axis_dim):
    kernel_len, in_chan, out_chan = weight_taps.shape
    backward_taps = lax.dot_general(
        deltas.reshape(-1, out_chan),
        weight_taps.reshape(kernel_len * in_chan, out_chan),
        (((1,), (1,)), ((), ())),
        preferred_element_type=jnp.float32,
    )
    backward_taps = backward_taps.reshape(deltas.shape[:-1] + (kernel_len * in_chan,))
    summed = None
    for tap_id in range(kernel_len):
        tap_part = backward_taps[..., tap_id * in_chan : (tap_id + 1) * in_chan]
        widths = [(0, 0)] * deltas.ndim
        widths[axis_dim] = (tap_id, kernel_len - 1 - tap_id)
        shifted = jnp.pad(tap_part, widths)
        summed = shifted if summed is None else summed + shifted
    return summed


def pad_along(values, axis_dim):
    widths = [(0, 0)] * values.ndim
    widths[axis_dim] = (2, 2)
    return jnp.pad(values, widths)


def crop_along(values, axis_dim):
    extent = values.shape[axis_dim] - 4
    return lax.slice_in_dim(values, 2, extent + 2, axis=axis_dim)


def section_forward(padded, context_parts, weights, axis_dim, extend):
    extent = padded.shape[axis_dim] - 4
    hidden_width = weights.shape[-1]
    own_inputs = lax.slice_in_dim(padded, 2, extent + 2, axis=axis_dim)
    hidden_own = own_inputs[..., :hidden_width].astype(jnp.float32)
    feat_padded = padded[..., hidden_width:]
    update_gate = jax.nn.sigmoid(
        conv_apply(padded, weights[0], extent, axis_dim) + context_parts[0].astype(jnp.float32)
    )
    reset_gate = jax.nn.sigmoid(
        conv_apply(padded, weights[1], extent, axis_dim) + context_parts[1].astype(jnp.float32)
    )
    reset_hidden = (reset_gate * hidden_own).astype(jnp.bfloat16)
    gated_padded = jnp.concatenate([extend(reset_hidden), feat_padded], axis=-1)
    candidate = jnp.tanh(
        conv_apply(gated_padded, weights[2], extent, axis_dim)
        + context_parts[2].astype(jnp.float32)
    )
    blended = (1.0 - update_gate) * hidden_own + update_gate * candidate
    return (blended, (update_gate, reset_gate, candidate, hidden_own, padded, gated_padded))


def section_backward(cotangent, stored, weights, axis_dim, fold_rims):
    update_gate, reset_gate, candidate, hidden_own, padded, gated_padded = stored
    hidden_width = weights.shape[-1]
    delta_cand = (cotangent * update_gate * (1.0 - candidate * candidate)).astype(jnp.bfloat16)
    grad_cand = conv_weight_grad(gated_padded, delta_cand, axis_dim)
    back_gated = fold_rims(conv_input_grad(delta_cand, weights[2][:, :hidden_width], axis_dim))
    delta_update = (
        cotangent * (candidate - hidden_own) * update_gate * (1.0 - update_gate)
    ).astype(jnp.bfloat16)
    delta_reset = (back_gated * hidden_own * reset_gate * (1.0 - reset_gate)).astype(jnp.bfloat16)
    grad_update = conv_weight_grad(padded, delta_update, axis_dim)
    grad_reset = conv_weight_grad(padded, delta_reset, axis_dim)
    grad_stack = jnp.stack([grad_update, grad_reset, grad_cand])
    back_inputs = conv_input_grad(
        delta_update, weights[0][:, :hidden_width], axis_dim
    ) + conv_input_grad(delta_reset, weights[1][:, :hidden_width], axis_dim)
    hidden_back = cotangent * (1.0 - update_gate) + back_gated * reset_gate + fold_rims(back_inputs)
    return (grad_stack, hidden_back)


def extend_gated(values):
    return with_halo(values, (("blk", 1),), 2)


def stripe_rims(values):
    extent = values.shape[1] - 4
    edge_terms = jnp.concatenate([values[:, :2], values[:, extent + 2 :]], axis=1)
    arrived = with_halo(edge_terms, (("blk", 1),), 2)
    own_terms = values[:, 2 : extent + 2]
    from_left = jnp.pad(arrived[:, :2], ((0, 0), (0, extent - 2), (0, 0)))
    from_right = jnp.pad(arrived[:, 6:], ((0, 0), (extent - 2, 0), (0, 0)))
    return own_terms + from_left + from_right


def on_device(left_feats, right_feats, offsets, hidden, context, gru_weights, hidden_grad):
    left_block = left_feats[0]
    right_block = right_feats[0]
    offset = offsets[0]
    stripe = lax.axis_index("blk")
    column_count = left_block.shape[1]
    empty_block = jnp.zeros_like(right_block)
    low_id = stripe - offset - 1
    high_id = stripe - offset
    shards = lax.all_gather(right_block, "blk", axis=1, tiled=True)
    shard_cols = shards.shape[1]

    def pick_one(slot_block, block_id):
        local_col = block_id * column_count
        usable = (local_col >= 0) & (local_col + column_count <= shard_cols)
        picked = lax.dynamic_slice_in_dim(
            shards, jnp.clip(local_col, 0, shard_cols - column_count), column_count, 1
        )
        return jnp.where(usable, picked, slot_block)

    low_block = pick_one(empty_block, low_id)
    high_block = pick_one(empty_block, high_id)
    window = jnp.concatenate([low_block, high_block], axis=1)
    scores = jnp.einsum("hxc,hjc->hxj", left_block, window, preferred_element_type=jnp.float32) * (
        1.0 / math.sqrt(left_block.shape[-1])
    )
    lookup = jnp.asarray(lookup_table(column_count, LEVELS, RADIUS))
    features = jnp.einsum("hxj,xjf->hxf", scores, lookup, precision=lax.Precision.HIGHEST).astype(
        jnp.bfloat16
    )
    context_parts = context[0]
    first_inputs = jnp.concatenate([hidden[0], features], axis=-1)
    first_padded = with_halo(first_inputs, (("blk", 1),), 2)
    first_new, first_stored = section_forward(
        first_padded, context_parts, gru_weights[0], 1, extend_gated
    )
    first_hidden = first_new.astype(jnp.bfloat16)
    second_inputs = jnp.concatenate([first_hidden, features], axis=-1)
    second_new, second_stored = section_forward(
        pad_along(second_inputs, 0),
        context_parts,
        gru_weights[1],
        0,
        functools.partial(pad_along, axis_dim=0),
    )
    second_grads, first_back = section_backward(
        hidden_grad[0], second_stored, gru_weights[1], 0, functools.partial(crop_along, axis_dim=0)
    )
    first_grads, hidden_back = section_backward(
        first_back, first_stored, gru_weights[0], 1, stripe_rims
    )
    grad_stack = lax.psum(jnp.stack([first_grads, second_grads]), ("pair", "blk"))
    return (second_new.astype(jnp.bfloat16)[None], grad_stack, hidden_back[None])


def solution(mesh):
    placed = (
        P("pair", None, "blk", None),
        P("pair", None, "blk", None),
        P("blk"),
        P("pair", None, "blk", None),
        P("pair", None, None, "blk", None),
        P(),
        P("pair", None, "blk", None),
    )
    return jax.shard_map(
        on_device,
        mesh=mesh,
        in_specs=placed,
        out_specs=(P("pair", None, "blk", None), P(), P("pair", None, "blk", None)),
        check_vma=False,
    )
```

profile of v0, /device:TPU:0, one launch (start us, length us, event | category | flops | bytes accessed | tf_op | source)
XLA Modules:
  0.0 494.4 jit_solution(1043420342084576107)
XLA Ops:
  8.6 129.2 %all-gather.3.cloned.1.call-done = bf16[1,64,256,256]{3,2,1,0:T(8,128)(2,1)} async-done(((bf16[1,64,32,256]{3,2,1,0:T(8,128)(2,1)}), bf16[1,64,256,256]{3,2,1,0:T(8,128)(2,1)}) %all-gather.3.cloned.1.call-update) | async-done | bytes 8388624 | tf_op jit(solution)/shard_map/all_gather | solution.py:174
  137.9 2.8 select_bitcast_fusion.1
  141.7 2.5 fusion.30
  146.6 4.5 collective-permute-start
  151.1 2.8 fusion.78
  155.8 2.7 fusion.76
  158.5 7.6 %concatenate.75 = bf16[64,32,820]{2,1,0:T(8,128)(2,1)} concatenate(bf16[64,32,164]{2,1,0:T(8,128)(2,1)} %get-tuple-element.86, bf16[64,32,164]{2,1,0:T(8,128)(2,1)} %get-tuple-element.87, bf16[64,32,128]{2,1,0:T(8,128)(2,1)S(1)} %bitcast.177, bf16[64,32,36]{2,1,0:T(8,128)(2,1)S(1)} %copy.20, bf16[64,32,164]{2,1,0:T(8,128)(2,1)S(1)} %get-tuple-element.56, ...), dimensions={2} | concatenate | bytes 6717440 | tf_op jit(solution)/shard_map/concatenate | solution.py:46
  166.1 4.4 fusion.34
  172.5 5.6 %collective-permute-start.2 = (bf16[64,2,128]{2,1,0:T(2,128)(2,1)}, bf16[64,2,128]{2,1,0:T(2,128)(2,1)}, u32[]{:S(2)}, u32[]{:S(2)}) collective-permute-start(bf16[64,2,128]{2,1,0:T(2,128)(2,1)} %get-tuple-element.78), channel_id=1, source_target_pairs={{0,1},{1,2},{2,3},{3,4},{4,5},{5,6},{6,7},{8,9},{9,10},{10,11},{11... | collective-permute-start | bytes 98312 | tf_op jit(solution)/shard_map/ppermute | solution.py:18
  201.7 7.6 %concatenate.90 = bf16[2048,820]{1,0:T(8,128)(2,1)} concatenate(bf16[2048,164]{1,0:T(8,128)(2,1)} %bitcast.185, bf16[2048,164]{1,0:T(8,128)(2,1)} %bitcast.186, bf16[2048,128]{1,0:T(8,128)(2,1)S(1)} %bitcast.178, bf16[2048,36]{1,0:T(8,128)(2,1)S(1)} %bitcast.173, bf16[2048,164]{1,0:T(8,128)(2,1)S(1)} %bitcast.184, bf16[2048,164]{1,0:T(8,128)(2,1)S(1)} %bitcast.183), dimensions={1} | concatenate | bytes 6717440 | tf_op jit(solution)/shard_map/concatenate | solution.py:46
  209.3 6.0 %copy.32 = bf16[820,2048]{1,0:T(8,128)(2,1)} copy(bf16[820,2048]{0,1:T(8,128)(2,1)} %bitcast.182) | data formatting | bytes 6717440 | tf_op jit(solution)/shard_map/dot_general | solution.py:73
  215.4 4.3 reshape.193
  221.2 2.8 fusion.75
  224.0 8.0 %concatenate.79 = bf16[64,32,820]{2,1,0:T(8,128)(2,1)} concatenate(bf16[64,32,164]{2,1,0:T(8,128)(2,1)} %get-tuple-element.54, bf16[64,32,164]{2,1,0:T(8,128)(2,1)} %get-tuple-element.53, bf16[64,32,164]{2,1,0:T(8,128)(2,1)} %get-tuple-element.52, bf16[64,32,164]{2,1,0:T(8,128)(2,1)S(1)} %get-tuple-element.51, bf16[64,32,164]{2,1,0:T(8,128)(2,1)S(1)} %get-tuple-element.50), dimensions={2} | concatenate | bytes 6717440 | tf_op jit(solution)/shard_map/concatenate | solution.py:46
  232.0 3.4 fusion.17
  239.0 2.4 pad_slice_fusion.3
  242.4 8.3 %concatenate.81 = bf16[64,32,820]{2,1,0:T(8,128)(2,1)} concatenate(bf16[64,32,164]{2,1,0:T(8,128)(2,1)} %get-tuple-element.73, bf16[64,32,164]{2,1,0:T(8,128)(2,1)} %get-tuple-element.71, bf16[64,32,128]{2,1,0:T(8,128)(2,1)} %copy-done.22, bf16[64,32,36]{2,1,0:T(8,128)(2,1)S(1)} %copy.20, bf16[64,32,164]{2,1,0:T(8,128)(2,1)} %get-tuple-element.72, ...), dimensions={2} | concatenate | bytes 6717440 | tf_op jit(solution)/shard_map/concatenate | solution.py:46
  250.6 4.5 fusion.16
  255.2 3.3 fusion.44
  261.1 8.5 %concatenate.83 = bf16[64,32,820]{2,1,0:T(8,128)(2,1)} concatenate(bf16[64,32,164]{2,1,0:T(8,128)(2,1)} %get-tuple-element.69, bf16[64,32,164]{2,1,0:T(8,128)(2,1)} %get-tuple-element.68, bf16[64,32,164]{2,1,0:T(8,128)(2,1)} %get-tuple-element.67, bf16[64,32,164]{2,1,0:T(8,128)(2,1)} %get-tuple-element.66, bf16[64,32,164]{2,1,0:T(8,128)(2,1)} %get-tuple-element.65), dimensions={2} | concatenate | bytes 6717440 | tf_op jit(solution)/shard_map/concatenate | solution.py:46
  269.7 5.3 %fusion.48 = (bf16[64,32,128]{2,1,0:T(8,128)(2,1)S(1)}, bf16[64,32,128]{2,1,0:T(8,128)(2,1)S(1)}, bf16[1,64,32,128]{3,2,1,0:T(8,128)(2,1)}) fusion(f32[64,32,128]{2,1,0:T(8,128)} %fusion.16, bf16[64,32,128]{2,1,0:T(8,128)(2,1)S(1)} %copy-done.23, f32[1,64,32,128]{3,2,1,0:T(8,128)} %param.14, bf16[1,3,64,32,128]{4,3,2,1,0:T(8,128)(2,1)} %param.12, ...), kind=kOutput, calls=%fused_computation.80 | convolution fusion | flops 434634752 | bytes 8287232 | tf_op jit(solution)/shard_map/dot_general | solution.py:59
  290.7 6.0 %copy.35 = bf16[820,2048]{1,0:T(8,128)(2,1)} copy(bf16[820,2048]{0,1:T(8,128)(2,1)} %bitcast.181) | data formatting | bytes 6717440 | tf_op jit(solution)/shard_map/dot_general | solution.py:73
  296.7 4.2 reshape.208
  300.8 6.0 %copy.34 = bf16[820,2048]{1,0:T(8,128)(2,1)} copy(bf16[820,2048]{0,1:T(8,128)(2,1)} %bitcast.180) | data formatting | bytes 6717440 | tf_op jit(solution)/shard_map/dot_general | solution.py:73
  306.8 4.4 reshape.204
  311.3 4.0 convolution_bitcast_fusion.1
  317.1 6.0 %copy.33 = bf16[820,2048]{1,0:T(8,128)(2,1)} copy(bf16[820,2048]{0,1:T(8,128)(2,1)} %bitcast.174) | data formatting | bytes 6717440 | tf_op jit(solution)/shard_map/dot_general | solution.py:73
  323.1 4.2 reshape.201
  328.6 4.5 collective-permute-start.4
  350.9 5.7 %collective-permute-start.6 = (f32[64,2,128]{2,1,0:T(2,128)S(1)}, f32[64,2,128]{2,1,0:T(2,128)S(1)}, u32[]{:S(2)}, u32[]{:S(2)}) collective-permute-start(f32[64,2,128]{2,1,0:T(2,128)S(1)} %add_add_fusion.2), channel_id=1, source_target_pairs={{0,1},{1,2},{2,3},{3,4},{4,5},{5,6},{6,7},{8,9},{9,10},{10,11},{11... | collective-permute-start | bytes 196616 | tf_op jit(solution)/shard_map/ppermute | solution.py:18
  360.4 122.4 %all-reduce.38.cloned.1.call-done = f32[2,3,5,164,128]{4,3,2,1,0:T(8,128)} async-done(((f32[2,3,5,164,128]{4,3,2,1,0:T(8,128)}), f32[2,3,5,164,128]{4,3,2,1,0:T(8,128)}) %all-reduce.38.cloned.1.call-update) | async-done | bytes 2519056 | tf_op jit(solution)/shard_map/psum | solution.py:216
  482.8 4.5 copy.36
  (201 shorter events, 79.9 us)
Async XLA Ops:
  7.2 133.5 %copy-start = (bf16[1,64,32,256]{3,2,1,0:T(8,128)(2,1)S(1)}, bf16[1,64,32,256]{3,2,1,0:T(8,128)(2,1)}, u32[]{:S(2)}) copy-start(bf16[1,64,32,256]{3,2,1,0:T(8,128)(2,1)} %param.8) | copy-start | bytes 3145732
  7.2 130.7 %all-gather.3.cloned.1.call-start = ((), (), s32[]{:S(2)}) async-start(), calls=%async_computation.1 | async-start | bytes 9437184 | tf_op jit(solution)/shard_map/all_gather | solution.py:174
  7.9 474.8 %all-reduce.38.cloned.1.call-start = ((), (), s32[]{:S(2)}) async-start(), calls=%async_computation | async-start | bytes 5160960 | tf_op jit(solution)/shard_map/psum | solution.py:216
  141.7 9.4 %copy-start.17 = (bf16[2,3,5,164,128]{4,0,3,2,1:T(2,128)(2,1)S(1)}, bf16[2,3,5,164,128]{4,0,3,2,1:T(2,128)(2,1)}, u32[]{:S(2)}) copy-start(bf16[2,3,5,164,128]{4,0,3,2,1:T(2,128)(2,1)} %param.13) | copy-start | bytes 3778564
  145.3 9.6 %collective-permute-start.1 = (bf16[64,2,164]{2,1,0:T(2,128)(2,1)S(1)}, bf16[64,2,164]{2,1,0:T(2,128)(2,1)S(1)}, u32[]{:S(2)}, u32[]{:S(2)}) collective-permute-start(bf16[64,2,164]{2,1,0:T(2,128)(2,1)S(1)} %get-tuple-element.76), channel_id=1, source_target_pairs={{1,0},{2,1},{3,2},{4,3},{5,4},{6,5},{7,6},{9,8},{10,9},{11,10},{12... | collective-permute-start | bytes 125960 | tf_op jit(solution)/shard_map/ppermute | solution.py:21
  146.6 8.3 %collective-permute-start = (bf16[64,2,164]{2,1,0:T(2,128)(2,1)S(1)}, bf16[64,2,164]{2,1,0:T(2,128)(2,1)S(1)}, u32[]{:S(2)}, u32[]{:S(2)}) collective-permute-start(bf16[64,2,164]{2,1,0:T(2,128)(2,1)S(1)} %get-tuple-element.77), channel_id=1, source_target_pairs={{0,1},{1,2},{2,3},{3,4},{4,5},{5,6},{6,7},{8,9},{9,10},{10,11},{11... | collective-permute-start | bytes 125960 | tf_op jit(solution)/shard_map/ppermute | solution.py:18
  166.1 12.1 %copy-start.34 = (bf16[1,1,5,164,128]{4,0,3,2,1:T(2,128)(2,1)S(1)}, bf16[1,1,5,164,128]{4,0,3,2,1:T(2,128)(2,1)}, u32[]{:S(2)}) copy-start(bf16[1,1,5,164,128]{4,0,3,2,1:T(2,128)(2,1)} %get-tuple-element.59) | copy-start | bytes 629764
  166.1 12.8 %copy-start.33 = (bf16[1,1,5,164,128]{4,0,3,2,1:T(2,128)(2,1)S(1)}, bf16[1,1,5,164,128]{4,0,3,2,1:T(2,128)(2,1)}, u32[]{:S(2)}) copy-start(bf16[1,1,5,164,128]{4,0,3,2,1:T(2,128)(2,1)} %get-tuple-element.60) | copy-start | bytes 629764
  170.6 12.0 %copy-start.46 = (bf16[64,32,128]{2,1,0:T(8,128)(2,1)}, bf16[64,32,128]{2,1,0:T(8,128)(2,1)S(1)}, u32[]{:S(2)}) copy-start(bf16[64,32,128]{2,1,0:T(8,128)(2,1)S(1)} %get-tuple-element.80) | copy-start | bytes 1572868
  170.6 9.8 %copy-start.32 = (bf16[1,1,5,164,128]{4,0,3,2,1:T(2,128)(2,1)S(1)}, bf16[1,1,5,164,128]{4,0,3,2,1:T(2,128)(2,1)}, u32[]{:S(2)}) copy-start(bf16[1,1,5,164,128]{4,0,3,2,1:T(2,128)(2,1)} %get-tuple-element.61) | copy-start | bytes 629764
  170.6 11.2 %copy-start.31 = (bf16[1,1,5,164,128]{4,0,3,2,1:T(2,128)(2,1)S(1)}, bf16[1,1,5,164,128]{4,0,3,2,1:T(2,128)(2,1)}, u32[]{:S(2)}) copy-start(bf16[1,1,5,164,128]{4,0,3,2,1:T(2,128)(2,1)} %get-tuple-element.62) | copy-start | bytes 629764
  171.2 48.4 %collective-permute-start.3 = (bf16[64,2,128]{2,1,0:T(2,128)(2,1)}, bf16[64,2,128]{2,1,0:T(2,128)(2,1)S(1)}, u32[]{:S(2)}, u32[]{:S(2)}) collective-permute-start(bf16[64,2,128]{2,1,0:T(2,128)(2,1)} %get-tuple-element.79), channel_id=1, source_target_pairs={{1,0},{2,1},{3,2},{4,3},{5,4},{6,5},{7,6},{9,8},{10,9},{11,10},{12... | collective-permute-start | bytes 98312 | tf_op jit(solution)/shard_map/ppermute | solution.py:21
  172.5 47.1 %collective-permute-start.2 = (bf16[64,2,128]{2,1,0:T(2,128)(2,1)}, bf16[64,2,128]{2,1,0:T(2,128)(2,1)}, u32[]{:S(2)}, u32[]{:S(2)}) collective-permute-start(bf16[64,2,128]{2,1,0:T(2,128)(2,1)} %get-tuple-element.78), channel_id=1, source_target_pairs={{0,1},{1,2},{2,3},{3,4},{4,5},{5,6},{6,7},{8,9},{9,10},{10,11},{11... | collective-permute-start | bytes 98312 | tf_op jit(solution)/shard_map/ppermute | solution.py:18
  178.2 5.0 %copy-start.30 = (bf16[1,1,5,164,128]{4,0,3,2,1:T(2,128)(2,1)S(1)}, bf16[1,1,5,164,128]{4,0,3,2,1:T(2,128)(2,1)}, u32[]{:S(2)}) copy-start(bf16[1,1,5,164,128]{4,0,3,2,1:T(2,128)(2,1)} %copy-done.29) | copy-start | bytes 629764
  179.0 5.0 %copy-start.28 = (bf16[1,1,5,164,128]{4,0,3,2,1:T(2,128)(2,1)S(1)}, bf16[1,1,5,164,128]{4,0,3,2,1:T(2,128)(2,1)}, u32[]{:S(2)}) copy-start(bf16[1,1,5,164,128]{4,0,3,2,1:T(2,128)(2,1)} %get-tuple-element.64) | copy-start | bytes 629764
  224.0 8.0 %copy-start.45 = (bf16[820,128,1]{1,0,2:T(8,128)(2,1)S(1)}, bf16[820,128,1]{1,0,2:T(8,128)(2,1)}, u32[]{:S(2)}) copy-start(bf16[820,128,1]{1,0,2:T(8,128)(2,1)} %reshape.226) | copy-start | bytes 629764
  237.9 47.4 %copy-start.11 = (f32[64,32,128]{2,1,0:T(8,128)}, f32[64,32,128]{2,1,0:T(8,128)S(1)}, u32[]{:S(2)}) copy-start(f32[64,32,128]{2,1,0:T(8,128)S(1)} %get-tuple-element.83) | copy-start | bytes 3145732
  250.6 4.5 copy-start.8
  250.6 4.5 copy-start.23
  250.6 4.5 copy-start.58
  269.7 6.1 %copy-start.52 = (bf16[5,128,128]{2,1,0:T(8,128)(2,1)S(1)}, bf16[5,128,128]{2,1,0:T(8,128)(2,1)}, u32[]{:S(2)}) copy-start(bf16[5,128,128]{2,1,0:T(8,128)(2,1)} %slice.398) | copy-start | bytes 491524
  275.0 5.6 %copy-start.39 = (bf16[64,32,128]{2,1,0:T(8,128)(2,1)}, bf16[64,32,128]{2,1,0:T(8,128)(2,1)S(1)}, u32[]{:S(2)}) copy-start(bf16[64,32,128]{2,1,0:T(8,128)(2,1)S(1)} %get-tuple-element.47) | copy-start | bytes 1572868
  323.1 10.1 %copy-start.48 = (bf16[5,128,128]{2,1,0:T(8,128)(2,1)S(1)}, bf16[5,128,128]{2,1,0:T(8,128)(2,1)}, u32[]{:S(2)}) copy-start(bf16[5,128,128]{2,1,0:T(8,128)(2,1)} %slice.423) | copy-start | bytes 491524
  327.3 14.4 %collective-permute-start.5 = (f32[64,2,128]{2,1,0:T(2,128)}, f32[64,2,128]{2,1,0:T(2,128)S(1)}, u32[]{:S(2)}, u32[]{:S(2)}) collective-permute-start(f32[64,2,128]{2,1,0:T(2,128)} %get-tuple-element.26), channel_id=1, source_target_pairs={{1,0},{2,1},{3,2},{4,3},{5,4},{6,5},{7,6},{9,8},{10,9},{11,10},{12... | collective-permute-start | bytes 196616 | tf_op jit(solution)/shard_map/ppermute | solution.py:21
  328.6 13.1 %collective-permute-start.4 = (f32[64,2,128]{2,1,0:T(2,128)S(1)}, f32[64,2,128]{2,1,0:T(2,128)S(1)}, u32[]{:S(2)}, u32[]{:S(2)}) collective-permute-start(f32[64,2,128]{2,1,0:T(2,128)S(1)} %get-tuple-element.25), channel_id=1, source_target_pairs={{0,1},{1,2},{2,3},{3,4},{4,5},{5,6},{6,7},{8,9},{9,10},{10,11},{11... | collective-permute-start | bytes 196616 | tf_op jit(solution)/shard_map/ppermute | solution.py:18
  349.4 9.0 %collective-permute-start.7 = (f32[64,2,128]{2,1,0:T(2,128)S(1)}, f32[64,2,128]{2,1,0:T(2,128)S(1)}, u32[]{:S(2)}, u32[]{:S(2)}) collective-permute-start(f32[64,2,128]{2,1,0:T(2,128)S(1)} %add_add_fusion.1), channel_id=1, source_target_pairs={{1,0},{2,1},{3,2},{4,3},{5,4},{6,5},{7,6},{9,8},{10,9},{11,10},{12... | collective-permute-start | bytes 196616 | tf_op jit(solution)/shard_map/ppermute | solution.py:21
  350.8 8.0 %copy-start.12 = (f32[64,32,128]{2,1,0:T(8,128)S(1)}, f32[64,32,128]{2,1,0:T(8,128)}, u32[]{:S(2)}) copy-start(f32[64,32,128]{2,1,0:T(8,128)} %copy-done.11) | copy-start | bytes 3145732
  350.9 8.0 %copy-start.14 = (f32[64,32,128]{2,1,0:T(8,128)S(1)}, f32[64,32,128]{2,1,0:T(8,128)}, u32[]{:S(2)}) copy-start(f32[64,32,128]{2,1,0:T(8,128)} %copy-done.13) | copy-start | bytes 3145732
  350.9 7.9 %copy-start.16 = (f32[64,36,128]{2,1,0:T(8,128)S(1)}, f32[64,36,128]{2,1,0:T(8,128)}, u32[]{:S(2)}) copy-start(f32[64,36,128]{2,1,0:T(8,128)} %pad_add_fusion) | copy-start | bytes 3538948
  350.9 7.9 %copy-start.26 = (f32[64,32,128]{2,1,0:T(8,128)S(1)}, f32[64,32,128]{2,1,0:T(8,128)}, u32[]{:S(2)}) copy-start(f32[64,32,128]{2,1,0:T(8,128)} %get-tuple-element.81) | copy-start | bytes 3145732
  350.9 7.9 %collective-permute-start.6 = (f32[64,2,128]{2,1,0:T(2,128)S(1)}, f32[64,2,128]{2,1,0:T(2,128)S(1)}, u32[]{:S(2)}, u32[]{:S(2)}) collective-permute-start(f32[64,2,128]{2,1,0:T(2,128)S(1)} %add_add_fusion.2), channel_id=1, source_target_pairs={{0,1},{1,2},{2,3},{3,4},{4,5},{5,6},{6,7},{8,9},{9,10},{10,11},{11... | collective-permute-start | bytes 196616 | tf_op jit(solution)/shard_map/ppermute | solution.py:18
  358.8 128.4 %copy-start.1 = (bf16[1,64,32,256]{3,2,1,0:T(8,128)(2,1)S(1)}, bf16[1,64,32,256]{3,2,1,0:T(8,128)(2,1)}, u32[]{:S(2)}) copy-start(bf16[1,64,32,256]{3,2,1,0:T(8,128)(2,1)} %param.8) | copy-start | bytes 3145732
  (38 other events, 80.8 us)
Sparse Core Ops, SparseCore 0:
  10.2 127.6 all-gather.2
  346.7 136.0 all-reduce.37
where the time goes:
time: 504 us; the launch traced here: 494 us
  waiting for transfers between devices  253 us (50%)
  local copies, waits for them, and re-layouts  141 us (28%)
  matrix products  41.8 us (8%)
  starting transfers between devices  25.7 us (5%)
  other arithmetic  17.8 us (4%)
  between operations  15.8 us (3%)
    all_gather x1, waiting for transfers between devices, on_device(): shards = lax.all_gather(right_block, 'blk', axis=1, tiled=True)  129 us
    psum x1, waiting for transfers between devices, on_device(): lax.psum(jnp.stack([first_grads, second_grads]), ('pair', 'blk'))  122 us
    concatenate x5, local copies, waits for them, and re-layouts, tap_stack(): jnp.concatenate([lax.slice_in_dim(padded, tap_id, tap_id + extent, axis=a...  40 us
    dot_general x4, local copies, waits for them, and re-layouts, conv_weight_grad(): lax.dot_general(flat_taps, flat_deltas, (((0,), (0,)), ((), ())), preferr...  24 us
    dot_general x6, matrix products, conv_apply(): jnp.dot(flat_taps, weight_taps.reshape(kernel_len * in_chan, out_chan), p...  23.4 us
    unnamed x133, local copies, waits for them, and re-layouts  22.1 us
    ppermute x4, starting transfers between devices, with_halo(): lax.ppermute(lax.slice_in_dim(block, block.shape[dim] - width, None, axis...  20.5 us
    another operation x4, local copies, waits for them, and re-layouts  17 us
  transfers between devices with their start and end apart: 10, of which 3 were waited for; matrix products, arithmetic and copies ran while one was open for 11% of the time, Pallas kernels for 0%

commit v1 on v0

--- a/solution.py
+++ b/solution.py
@@ -213,7 +213,8 @@
     first_grads, hidden_back = section_backward(
         first_back, first_stored, gru_weights[0], 1, stripe_rims
     )
-    grad_stack = lax.psum(jnp.stack([first_grads, second_grads]), ("pair", "blk"))
+    half = lax.psum(jnp.stack([first_grads, second_grads]), "blk")
+    grad_stack = lax.psum(half, "pair")
     return (second_new.astype(jnp.bfloat16)[None], grad_stack, hidden_back[None])
 
 

time: 504 us -> 537 us (1.065)
  waiting for transfers between devices: 253 us -> 289 us
    psum x1 -> x2, waiting for transfers between devices: 122 us -> 159 us  [the longest x1 111 us: on_device(): half = lax.psum(jnp.stack([first_grads, second_grads]), 'blk')]
    unnamed x133 -> x125, local copies, waits for them, and re-layouts: 22.1 us -> 20.6 us
  transfers between devices with their start and end apart: 10 -> 11, of which waited for: 3 -> 3; matrix products, arithmetic and copies ran while one was open for 11% -> 10% of each run, Pallas kernels for 0% -> 0%
where the time goes in v1:
time: 537 us; the launch traced here: 527 us
  waiting for transfers between devices  289 us (54%)
  local copies, waits for them, and re-layouts  137 us (26%)
  matrix products  44 us (8%)
  starting transfers between devices  25.3 us (5%)
  other arithmetic  16.7 us (3%)
  between operations  15.6 us (3%)
    all_gather x1, waiting for transfers between devices, on_device(): shards = lax.all_gather(right_block, 'blk', axis=1, tiled=True)  129 us
    psum x1, waiting for transfers between devices, on_device(): half = lax.psum(jnp.stack([first_grads, second_grads]), 'blk')  111 us
    psum x1, waiting for transfers between devices, on_device(): grad_stack = lax.psum(half, 'pair')  47.3 us
    concatenate x5, local copies, waits for them, and re-layouts, tap_stack(): jnp.concatenate([lax.slice_in_dim(padded, tap_id, tap_id + extent, axis=a...  40 us
    dot_general x4, local copies, waits for them, and re-layouts, conv_weight_grad(): lax.dot_general(flat_taps, flat_deltas, (((0,), (0,)), ((), ())), preferr...  24.6 us
    dot_general x6, matrix products, conv_apply(): jnp.dot(flat_taps, weight_taps.reshape(kernel_len * in_chan, out_chan), p...  23.4 us
    unnamed x125, local copies, waits for them, and re-layouts  20.6 us
    ppermute x4, starting transfers between devices, with_halo(): lax.ppermute(lax.slice_in_dim(block, block.shape[dim] - width, None, axis...  19.8 us
  transfers between devices with their start and end apart: 11, of which 3 were waited for; matrix products, arithmetic and copies ran while one was open for 10% of the time, Pallas kernels for 0%

profile of v1, /device:TPU:0, one launch (start us, length us, event | category | flops | bytes accessed | tf_op | source)
XLA Modules:
  0.0 526.7 jit_solution(5640864698744101994)
XLA Ops:
  8.6 129.2 %all-gather.3.cloned.1.call-done = bf16[1,64,256,256]{3,2,1,0:T(8,128)(2,1)} async-done(((bf16[1,64,32,256]{3,2,1,0:T(8,128)(2,1)}), bf16[1,64,256,256]{3,2,1,0:T(8,128)(2,1)}) %all-gather.3.cloned.1.call-update) | async-done | bytes 8388624 | tf_op jit(solution)/shard_map/all_gather | solution.py:174
  137.9 2.8 select_bitcast_fusion.1
  146.6 4.5 collective-permute-start
  151.1 2.9 fusion.78
  155.8 2.7 fusion.76
  158.5 7.6 %concatenate.75 = bf16[64,32,820]{2,1,0:T(8,128)(2,1)} concatenate(bf16[64,32,164]{2,1,0:T(8,128)(2,1)} %get-tuple-element.86, bf16[64,32,164]{2,1,0:T(8,128)(2,1)} %get-tuple-element.87, bf16[64,32,128]{2,1,0:T(8,128)(2,1)S(1)} %bitcast.177, bf16[64,32,36]{2,1,0:T(8,128)(2,1)S(1)} %copy.20, bf16[64,32,164]{2,1,0:T(8,128)(2,1)S(1)} %get-tuple-element.56, ...), dimensions={2} | concatenate | bytes 6717440 | tf_op jit(solution)/shard_map/concatenate | solution.py:46
  166.2 4.4 fusion.34
  172.6 5.6 %collective-permute-start.2 = (bf16[64,2,128]{2,1,0:T(2,128)(2,1)}, bf16[64,2,128]{2,1,0:T(2,128)(2,1)}, u32[]{:S(2)}, u32[]{:S(2)}) collective-permute-start(bf16[64,2,128]{2,1,0:T(2,128)(2,1)} %get-tuple-element.78), channel_id=1, source_target_pairs={{0,1},{1,2},{2,3},{3,4},{4,5},{5,6},{6,7},{8,9},{9,10},{10,11},{11... | collective-permute-start | bytes 98312 | tf_op jit(solution)/shard_map/ppermute | solution.py:18
  198.0 7.6 %concatenate.90 = bf16[2048,820]{1,0:T(8,128)(2,1)} concatenate(bf16[2048,164]{1,0:T(8,128)(2,1)} %bitcast.185, bf16[2048,164]{1,0:T(8,128)(2,1)} %bitcast.186, bf16[2048,128]{1,0:T(8,128)(2,1)S(1)} %bitcast.178, bf16[2048,36]{1,0:T(8,128)(2,1)S(1)} %bitcast.173, bf16[2048,164]{1,0:T(8,128)(2,1)S(1)} %bitcast.184, bf16[2048,164]{1,0:T(8,128)(2,1)S(1)} %bitcast.183), dimensions={1} | concatenate | bytes 6717440 | tf_op jit(solution)/shard_map/concatenate | solution.py:46
  205.6 6.1 %copy.32 = bf16[820,2048]{1,0:T(8,128)(2,1)} copy(bf16[820,2048]{0,1:T(8,128)(2,1)} %bitcast.182) | data formatting | bytes 6717440 | tf_op jit(solution)/shard_map/dot_general | solution.py:73
  211.7 4.2 reshape.193
  217.5 2.8 fusion.75
  220.3 7.9 %concatenate.79 = bf16[64,32,820]{2,1,0:T(8,128)(2,1)} concatenate(bf16[64,32,164]{2,1,0:T(8,128)(2,1)} %get-tuple-element.54, bf16[64,32,164]{2,1,0:T(8,128)(2,1)} %get-tuple-element.53, bf16[64,32,164]{2,1,0:T(8,128)(2,1)} %get-tuple-element.52, bf16[64,32,164]{2,1,0:T(8,128)(2,1)S(1)} %get-tuple-element.51, bf16[64,32,164]{2,1,0:T(8,128)(2,1)S(1)} %get-tuple-element.50), dimensions={2} | concatenate | bytes 6717440 | tf_op jit(solution)/shard_map/concatenate | solution.py:46
  228.3 3.4 fusion.17
  238.6 8.3 %concatenate.81 = bf16[64,32,820]{2,1,0:T(8,128)(2,1)} concatenate(bf16[64,32,164]{2,1,0:T(8,128)(2,1)} %get-tuple-element.73, bf16[64,32,164]{2,1,0:T(8,128)(2,1)} %get-tuple-element.71, bf16[64,32,128]{2,1,0:T(8,128)(2,1)} %copy-done.21, bf16[64,32,36]{2,1,0:T(8,128)(2,1)S(1)} %copy.20, bf16[64,32,164]{2,1,0:T(8,128)(2,1)} %get-tuple-element.72, ...), dimensions={2} | concatenate | bytes 6717440 | tf_op jit(solution)/shard_map/concatenate | solution.py:46
  246.9 4.5 fusion.16
  251.4 3.3 fusion.44
  257.4 8.5 %concatenate.83 = bf16[64,32,820]{2,1,0:T(8,128)(2,1)} concatenate(bf16[64,32,164]{2,1,0:T(8,128)(2,1)} %get-tuple-element.69, bf16[64,32,164]{2,1,0:T(8,128)(2,1)} %get-tuple-element.68, bf16[64,32,164]{2,1,0:T(8,128)(2,1)} %get-tuple-element.67, bf16[64,32,164]{2,1,0:T(8,128)(2,1)} %get-tuple-element.66, bf16[64,32,164]{2,1,0:T(8,128)(2,1)} %get-tuple-element.65), dimensions={2} | concatenate | bytes 6717440 | tf_op jit(solution)/shard_map/concatenate | solution.py:46
  265.9 5.3 %fusion.48 = (bf16[64,32,128]{2,1,0:T(8,128)(2,1)S(1)}, bf16[64,32,128]{2,1,0:T(8,128)(2,1)S(1)}, bf16[1,64,32,128]{3,2,1,0:T(8,128)(2,1)}) fusion(f32[64,32,128]{2,1,0:T(8,128)} %fusion.16, bf16[64,32,128]{2,1,0:T(8,128)(2,1)S(1)} %copy-done.22, f32[1,64,32,128]{3,2,1,0:T(8,128)} %param.14, bf16[1,3,64,32,128]{4,3,2,1,0:T(8,128)(2,1)} %param.12, ...), kind=kOutput, calls=%fused_computation.80 | convolution fusion | flops 434634752 | bytes 8287232 | tf_op jit(solution)/shard_map/dot_general | solution.py:59
  285.8 6.5 %copy.35 = bf16[820,2048]{1,0:T(8,128)(2,1)} copy(bf16[820,2048]{0,1:T(8,128)(2,1)} %bitcast.181) | data formatting | bytes 6717440 | tf_op jit(solution)/shard_map/dot_general | solution.py:73
  292.3 4.2 reshape.208
  296.5 6.0 %copy.34 = bf16[820,2048]{1,0:T(8,128)(2,1)} copy(bf16[820,2048]{0,1:T(8,128)(2,1)} %bitcast.180) | data formatting | bytes 6717440 | tf_op jit(solution)/shard_map/dot_general | solution.py:73
  302.5 4.5 reshape.204
  307.0 3.2 convolution_bitcast_fusion.1
  312.0 6.0 %copy.33 = bf16[820,2048]{1,0:T(8,128)(2,1)} copy(bf16[820,2048]{0,1:T(8,128)(2,1)} %bitcast.174) | data formatting | bytes 6717440 | tf_op jit(solution)/shard_map/dot_general | solution.py:73
  318.0 4.2 reshape.201
  323.8 4.5 collective-permute-start.4
  328.4 3.0 convolution_bitcast_fusion
  343.2 111.4 %all-reduce.39.cloned.1.call-done = f32[2,3,5,164,128]{4,3,2,1,0:T(8,128)} async-done(((f32[2,3,5,164,128]{4,3,2,1,0:T(8,128)}), f32[2,3,5,164,128]{4,3,2,1,0:T(8,128)}) %all-reduce.39.cloned.1.call-update) | async-done | bytes 2519056 | tf_op jit(solution)/shard_map/psum | solution.py:216
  459.7 5.1 collective-permute-start.6
  468.1 47.3 %all-reduce.41.cloned.1.call-done = f32[2,3,5,164,128]{4,3,2,1,0:T(8,128)} async-done(((f32[2,3,5,164,128]{4,3,2,1,0:T(8,128)}), f32[2,3,5,164,128]{4,3,2,1,0:T(8,128)}) %all-reduce.41.cloned.1.call-update) | async-done | bytes 2519056 | tf_op jit(solution)/shard_map/psum | solution.py:217
  515.4 4.5 copy.36
  (196 shorter events, 79.0 us)
Async XLA Ops:
  7.2 133.5 %copy-start = (bf16[1,64,32,256]{3,2,1,0:T(8,128)(2,1)S(1)}, bf16[1,64,32,256]{3,2,1,0:T(8,128)(2,1)}, u32[]{:S(2)}) copy-start(bf16[1,64,32,256]{3,2,1,0:T(8,128)(2,1)} %param.8) | copy-start | bytes 3145732
  7.2 130.7 %all-gather.3.cloned.1.call-start = ((), (), s32[]{:S(2)}) async-start(), calls=%async_computation.2 | async-start | bytes 9437184 | tf_op jit(solution)/shard_map/all_gather | solution.py:174
  7.9 446.7 %all-reduce.39.cloned.1.call-start = ((), (), s32[]{:S(2)}) async-start(), calls=%async_computation | async-start | bytes 5160960 | tf_op jit(solution)/shard_map/psum | solution.py:216
  141.7 9.4 %copy-start.15 = (bf16[2,3,5,164,128]{4,0,3,2,1:T(2,128)(2,1)S(1)}, bf16[2,3,5,164,128]{4,0,3,2,1:T(2,128)(2,1)}, u32[]{:S(2)}) copy-start(bf16[2,3,5,164,128]{4,0,3,2,1:T(2,128)(2,1)} %param.13) | copy-start | bytes 3778564
  145.3 9.6 %collective-permute-start.1 = (bf16[64,2,164]{2,1,0:T(2,128)(2,1)S(1)}, bf16[64,2,164]{2,1,0:T(2,128)(2,1)S(1)}, u32[]{:S(2)}, u32[]{:S(2)}) collective-permute-start(bf16[64,2,164]{2,1,0:T(2,128)(2,1)S(1)} %get-tuple-element.76), channel_id=1, source_target_pairs={{1,0},{2,1},{3,2},{4,3},{5,4},{6,5},{7,6},{9,8},{10,9},{11,10},{12... | collective-permute-start | bytes 125960 | tf_op jit(solution)/shard_map/ppermute | solution.py:21
  146.6 8.3 %collective-permute-start = (bf16[64,2,164]{2,1,0:T(2,128)(2,1)S(1)}, bf16[64,2,164]{2,1,0:T(2,128)(2,1)S(1)}, u32[]{:S(2)}, u32[]{:S(2)}) collective-permute-start(bf16[64,2,164]{2,1,0:T(2,128)(2,1)S(1)} %get-tuple-element.77), channel_id=1, source_target_pairs={{0,1},{1,2},{2,3},{3,4},{4,5},{5,6},{6,7},{8,9},{9,10},{10,11},{11... | collective-permute-start | bytes 125960 | tf_op jit(solution)/shard_map/ppermute | solution.py:18
  166.2 12.1 %copy-start.33 = (bf16[1,1,5,164,128]{4,0,3,2,1:T(2,128)(2,1)S(1)}, bf16[1,1,5,164,128]{4,0,3,2,1:T(2,128)(2,1)}, u32[]{:S(2)}) copy-start(bf16[1,1,5,164,128]{4,0,3,2,1:T(2,128)(2,1)} %get-tuple-element.59) | copy-start | bytes 629764
  166.2 12.8 %copy-start.32 = (bf16[1,1,5,164,128]{4,0,3,2,1:T(2,128)(2,1)S(1)}, bf16[1,1,5,164,128]{4,0,3,2,1:T(2,128)(2,1)}, u32[]{:S(2)}) copy-start(bf16[1,1,5,164,128]{4,0,3,2,1:T(2,128)(2,1)} %get-tuple-element.60) | copy-start | bytes 629764
  170.6 11.9 %copy-start.44 = (bf16[64,32,128]{2,1,0:T(8,128)(2,1)}, bf16[64,32,128]{2,1,0:T(8,128)(2,1)S(1)}, u32[]{:S(2)}) copy-start(bf16[64,32,128]{2,1,0:T(8,128)(2,1)S(1)} %get-tuple-element.80) | copy-start | bytes 1572868
  170.6 9.8 %copy-start.31 = (bf16[1,1,5,164,128]{4,0,3,2,1:T(2,128)(2,1)S(1)}, bf16[1,1,5,164,128]{4,0,3,2,1:T(2,128)(2,1)}, u32[]{:S(2)}) copy-start(bf16[1,1,5,164,128]{4,0,3,2,1:T(2,128)(2,1)} %get-tuple-element.61) | copy-start | bytes 629764
  170.6 11.2 %copy-start.30 = (bf16[1,1,5,164,128]{4,0,3,2,1:T(2,128)(2,1)S(1)}, bf16[1,1,5,164,128]{4,0,3,2,1:T(2,128)(2,1)}, u32[]{:S(2)}) copy-start(bf16[1,1,5,164,128]{4,0,3,2,1:T(2,128)(2,1)} %get-tuple-element.62) | copy-start | bytes 629764
  171.3 44.6 %collective-permute-start.3 = (bf16[64,2,128]{2,1,0:T(2,128)(2,1)}, bf16[64,2,128]{2,1,0:T(2,128)(2,1)S(1)}, u32[]{:S(2)}, u32[]{:S(2)}) collective-permute-start(bf16[64,2,128]{2,1,0:T(2,128)(2,1)} %get-tuple-element.79), channel_id=1, source_target_pairs={{1,0},{2,1},{3,2},{4,3},{5,4},{6,5},{7,6},{9,8},{10,9},{11,10},{12... | collective-permute-start | bytes 98312 | tf_op jit(solution)/shard_map/ppermute | solution.py:21
  172.6 43.4 %collective-permute-start.2 = (bf16[64,2,128]{2,1,0:T(2,128)(2,1)}, bf16[64,2,128]{2,1,0:T(2,128)(2,1)}, u32[]{:S(2)}, u32[]{:S(2)}) collective-permute-start(bf16[64,2,128]{2,1,0:T(2,128)(2,1)} %get-tuple-element.78), channel_id=1, source_target_pairs={{0,1},{1,2},{2,3},{3,4},{4,5},{5,6},{6,7},{8,9},{9,10},{10,11},{11... | collective-permute-start | bytes 98312 | tf_op jit(solution)/shard_map/ppermute | solution.py:18
  220.3 8.0 %copy-start.43 = (bf16[820,128,1]{1,0,2:T(8,128)(2,1)S(1)}, bf16[820,128,1]{1,0,2:T(8,128)(2,1)}, u32[]{:S(2)}) copy-start(bf16[820,128,1]{1,0,2:T(8,128)(2,1)} %reshape.226) | copy-start | bytes 629764
  234.1 47.4 %copy-start.9 = (f32[64,32,128]{2,1,0:T(8,128)}, f32[64,32,128]{2,1,0:T(8,128)S(1)}, u32[]{:S(2)}) copy-start(f32[64,32,128]{2,1,0:T(8,128)S(1)} %get-tuple-element.83) | copy-start | bytes 3145732
  246.9 4.5 copy-start.54
  265.9 6.1 %copy-start.48 = (bf16[5,128,128]{2,1,0:T(8,128)(2,1)S(1)}, bf16[5,128,128]{2,1,0:T(8,128)(2,1)}, u32[]{:S(2)}) copy-start(bf16[5,128,128]{2,1,0:T(8,128)(2,1)} %slice.398) | copy-start | bytes 491524
  271.2 5.5 %copy-start.38 = (bf16[64,32,128]{2,1,0:T(8,128)(2,1)}, bf16[64,32,128]{2,1,0:T(8,128)(2,1)S(1)}, u32[]{:S(2)}) copy-start(bf16[64,32,128]{2,1,0:T(8,128)(2,1)S(1)} %get-tuple-element.47) | copy-start | bytes 1572868
  285.8 48.8 %copy-start.13 = (f32[64,36,128]{2,1,0:T(8,128)}, f32[64,36,128]{2,1,0:T(8,128)S(1)}, u32[]{:S(2)}) copy-start(f32[64,36,128]{2,1,0:T(8,128)S(1)} %pad_add_fusion) | copy-start | bytes 3538948
  318.0 10.3 %copy-start.37 = (bf16[64,32,128]{2,1,0:T(8,128)(2,1)S(1)}, bf16[64,32,128]{2,1,0:T(8,128)(2,1)}, u32[]{:S(2)}) copy-start(bf16[64,32,128]{2,1,0:T(8,128)(2,1)} %copy-done.36) | copy-start | bytes 1572868
  322.2 9.2 %copy-start.8 = (bf16[5,164,2048]{2,1,0:T(8,128)(2,1)S(1)}, bf16[5,164,2048]{2,1,0:T(8,128)(2,1)}, u32[]{:S(2)}) copy-start(bf16[5,164,2048]{2,1,0:T(8,128)(2,1)} %reshape.201) | copy-start | bytes 10076164
  322.3 9.2 %copy-start.19 = (bf16[64,32,128]{2,1,0:T(8,128)(2,1)S(1)}, bf16[64,32,128]{2,1,0:T(8,128)(2,1)}, u32[]{:S(2)}) copy-start(bf16[64,32,128]{2,1,0:T(8,128)(2,1)} %copy-done.18) | copy-start | bytes 1572868
  322.3 12.4 %collective-permute-start.5 = (f32[64,2,128]{2,1,0:T(2,128)}, f32[64,2,128]{2,1,0:T(2,128)S(1)}, u32[]{:S(2)}, u32[]{:S(2)}) collective-permute-start(f32[64,2,128]{2,1,0:T(2,128)} %get-tuple-element.26), channel_id=1, source_target_pairs={{1,0},{2,1},{3,2},{4,3},{5,4},{6,5},{7,6},{9,8},{10,9},{11,10},{12... | collective-permute-start | bytes 196616 | tf_op jit(solution)/shard_map/ppermute | solution.py:21
  323.8 10.8 %collective-permute-start.4 = (f32[64,2,128]{2,1,0:T(2,128)S(1)}, f32[64,2,128]{2,1,0:T(2,128)S(1)}, u32[]{:S(2)}, u32[]{:S(2)}) collective-permute-start(f32[64,2,128]{2,1,0:T(2,128)S(1)} %get-tuple-element.25), channel_id=1, source_target_pairs={{0,1},{1,2},{2,3},{3,4},{4,5},{5,6},{6,7},{8,9},{9,10},{10,11},{11... | collective-permute-start | bytes 196616 | tf_op jit(solution)/shard_map/ppermute | solution.py:18
  339.2 176.3 %all-reduce.41.cloned.1.call-start = ((), (), s32[]{:S(2)}) async-start(), calls=%async_computation.1 | async-start | bytes 5160960 | tf_op jit(solution)/shard_map/psum | solution.py:217
  458.2 8.3 %collective-permute-start.7 = (f32[64,2,128]{2,1,0:T(2,128)S(1)}, f32[64,2,128]{2,1,0:T(2,128)S(1)}, u32[]{:S(2)}, u32[]{:S(2)}) collective-permute-start(f32[64,2,128]{2,1,0:T(2,128)S(1)} %add_add_fusion.1), channel_id=1, source_target_pairs={{1,0},{2,1},{3,2},{4,3},{5,4},{6,5},{7,6},{9,8},{10,9},{11,10},{12... | collective-permute-start | bytes 196616 | tf_op jit(solution)/shard_map/ppermute | solution.py:21
  459.7 6.9 %copy-start.10 = (f32[64,32,128]{2,1,0:T(8,128)S(1)}, f32[64,32,128]{2,1,0:T(8,128)}, u32[]{:S(2)}) copy-start(f32[64,32,128]{2,1,0:T(8,128)} %copy-done.9) | copy-start | bytes 3145732
  459.7 6.9 %copy-start.12 = (f32[64,32,128]{2,1,0:T(8,128)S(1)}, f32[64,32,128]{2,1,0:T(8,128)}, u32[]{:S(2)}) copy-start(f32[64,32,128]{2,1,0:T(8,128)} %copy-done.11) | copy-start | bytes 3145732
  459.7 6.9 %copy-start.14 = (f32[64,36,128]{2,1,0:T(8,128)S(1)}, f32[64,36,128]{2,1,0:T(8,128)}, u32[]{:S(2)}) copy-start(f32[64,36,128]{2,1,0:T(8,128)} %copy-done.13) | copy-start | bytes 3538948
  459.7 6.9 %copy-start.25 = (f32[64,32,128]{2,1,0:T(8,128)S(1)}, f32[64,32,128]{2,1,0:T(8,128)}, u32[]{:S(2)}) copy-start(f32[64,32,128]{2,1,0:T(8,128)} %get-tuple-element.81) | copy-start | bytes 3145732
  459.7 6.8 %collective-permute-start.6 = (f32[64,2,128]{2,1,0:T(2,128)S(1)}, f32[64,2,128]{2,1,0:T(2,128)S(1)}, u32[]{:S(2)}, u32[]{:S(2)}) collective-permute-start(f32[64,2,128]{2,1,0:T(2,128)S(1)} %add_add_fusion.2), channel_id=1, source_target_pairs={{0,1},{1,2},{2,3},{3,4},{4,5},{5,6},{6,7},{8,9},{9,10},{10,11},{11... | collective-permute-start | bytes 196616 | tf_op jit(solution)/shard_map/ppermute | solution.py:18
  466.6 53.3 %copy-start.1 = (bf16[1,64,32,256]{3,2,1,0:T(8,128)(2,1)S(1)}, bf16[1,64,32,256]{3,2,1,0:T(8,128)(2,1)}, u32[]{:S(2)}) copy-start(bf16[1,64,32,256]{3,2,1,0:T(8,128)(2,1)} %param.8) | copy-start | bytes 3145732
  (35 other events, 73.7 us)
Sparse Core Ops, SparseCore 0:
  10.2 127.6 all-gather.2
  339.3 115.3 all-reduce.38
  457.0 58.3 all-reduce.40
